TPU v7x, 128 devices: a whole 4x4x4 slice. The times are simulated.
128 devices in a mesh: fsdp: 16 (over z, x_lo, core), tp: 8 (over x_hi, y).
Axes of the slice: x: 4 (x_hi: 2, x_lo: 2; x = x_hi * 2 + x_lo), y: 4, z: 4, core: 2. Of those that a mesh axis runs over, the one named last changes fastest.
Arguments:
- states: bfloat16 [512, 4, 8192], P('fsdp'), may hold values from -6 to 6
- norm_gain: float32 [8192], replicated, may hold values from 0.5 to 1.5
- query_base: bfloat16 [8192, 8192], P(('fsdp', 'tp')), may hold values from -0.0625 to 0.0625
- key_base: bfloat16 [8192, 1024], P(('fsdp', 'tp')), may hold values from -0.0625 to 0.0625
- value_base: bfloat16 [8192, 1024], P(('fsdp', 'tp')), may hold values from -0.0625 to 0.0625
- output_base: bfloat16 [8192, 8192], P(('fsdp', 'tp')), may hold values from -0.5 to 0.5
- query_down: bfloat16 [4, 8192, 64], P(None, ('fsdp', 'tp')), may hold values from -0.0625 to 0.0625
- query_up: bfloat16 [4, 64, 8192], replicated, may hold values from -0.75 to 0.75
- key_down: bfloat16 [4, 8192, 64], P(None, ('fsdp', 'tp')), may hold values from -0.0625 to 0.0625
- key_up: bfloat16 [4, 64, 1024], replicated, may hold values from -0.75 to 0.75
- value_down: bfloat16 [4, 8192, 64], P(None, ('fsdp', 'tp')), may hold values from -0.0625 to 0.0625
- value_up: bfloat16 [4, 64, 1024], replicated, may hold values from -0.75 to 0.75
- output_down: bfloat16 [4, 8192, 64], P(None, ('fsdp', 'tp')), may hold values from -0.5 to 0.5
- output_up: bfloat16 [4, 64, 8192], replicated, may hold values from -0.75 to 0.75
- adapter_layer: int32 [1], replicated, may hold values from 0 to 3
- kv_lengths: int32 [512], P('fsdp'), may hold values from 8 to 512
- cache_keys: bfloat16 [512, 512, 8, 128], P('fsdp', None, 'tp'), may hold values from -320 to 320
- cache_values: bfloat16 [512, 512, 8, 128], P('fsdp', None, 'tp'), may hold values from -6 to 6
Outputs:
- layer_update: bfloat16 [512, 4, 8192], P('fsdp', None, 'tp')
Inputs may be any that keep to these rules, and one draw needn't show every extreme that they name: `kv_lengths`: slots at and beyond a sequence's length hold no cached position.
All inputs are finite; a program needn't handle non-finite values.
Results may differ from a plain program's by a relative error of at most 0.012.
The roundings to bfloat16 on the way count: a program that leaves them out, or rounds other values in their place, can miss the bound.
Values may be sent and summed in bfloat16 or wider, within the bound.
A program may use at most 128 MiB of HBM per device.

v0:
```python
import jax
import jax.numpy as jnp
from jax import lax
from jax.sharding import PartitionSpec as P

HQ = 64
KVH = 8
DH = 128
rope_theta = 1000000.0
low_rank_scale = 0.5
epsilon = 1e-06


def sent_to_all(array, axis):
    copies = jnp.broadcast_to(array, (lax.axis_size(axis), *array.shape))
    return lax.all_to_all(copies, axis, split_axis=0, concat_axis=0, tiled=True)


def joined_along(tiles, dim):
    tiles = jnp.moveaxis(tiles, 0, dim)
    shape = tiles.shape
    return tiles.reshape(*shape[:dim], shape[dim] * shape[dim + 1], *shape[dim + 2 :])


def collect(array, axis, dim):
    tiles = sent_to_all(array, axis)
    return joined_along(tiles, dim)


def merge_rows(frozen_base_rows, down_stack, up_stack, adapter_slot):
    down_rows = lax.dynamic_index_in_dim(down_stack, adapter_slot, 0, keepdims=False)
    up_projection_rows = lax.dynamic_index_in_dim(up_stack, adapter_slot, 0, keepdims=False)
    low_rank_delta = jnp.dot(down_rows, up_projection_rows, preferred_element_type=jnp.float32)
    return (frozen_base_rows.astype(jnp.float32) + low_rank_scale * low_rank_delta).astype(
        jnp.bfloat16
    )


def normalize(states, norm_gain):
    widened = states.astype(jnp.float32)
    squared_average = jnp.mean(widened * widened, axis=-1, keepdims=True)
    return (widened * lax.rsqrt(squared_average + epsilon) * norm_gain).astype(jnp.bfloat16)


def rotate(vectors, positions):
    head_dim = vectors.shape[-1]
    half_dim = head_dim // 2
    frequency = rope_theta ** (-2.0 * jnp.arange(half_dim, dtype=jnp.float32) / head_dim)
    rotation_phases = positions[:, :, None] * frequency[None, None, :]
    cosine_table = jnp.concatenate((jnp.cos(rotation_phases), jnp.cos(rotation_phases)), -1)[
        :, :, None, :
    ]
    sine_table = jnp.concatenate((jnp.sin(rotation_phases), jnp.sin(rotation_phases)), -1)[
        :, :, None, :
    ]
    turned = jnp.concatenate((-vectors[..., half_dim:], vectors[..., :half_dim]), -1)
    return vectors * cosine_table + turned * sine_table


def attend(queries, keys_new, values_new, cache_k, cache_v, lengths):
    seq_count, step_count, head_count, head_dim = queries.shape
    kv_count = keys_new.shape[2]
    grouped = queries.reshape(seq_count, step_count, kv_count, head_count // kv_count, head_dim)
    score_scale = head_dim ** (-0.5)
    old_scores = (
        jnp.einsum("bskgd,blkd->bskgl", grouped, cache_k, preferred_element_type=jnp.float32)
        * score_scale
    )
    new_scores = (
        jnp.einsum("bskgd,btkd->bskgt", grouped, keys_new, preferred_element_type=jnp.float32)
        * score_scale
    )
    live_slots = jnp.arange(cache_k.shape[1], dtype=jnp.int32)[None, :] < lengths[:, None]
    old_scores = jnp.where(live_slots[:, None, None, None, :], old_scores, -1e30)
    causal = jnp.arange(step_count)[:, None] >= jnp.arange(step_count)[None, :]
    new_scores = jnp.where(causal[None, :, None, None, :], new_scores, -1e30)
    highest = jnp.maximum(jnp.max(old_scores, -1), jnp.max(new_scores, -1))[..., None]
    old_exp = jnp.exp(old_scores - highest)
    new_exp = jnp.exp(new_scores - highest)
    denominator = jnp.sum(old_exp, -1, keepdims=True) + jnp.sum(new_exp, -1, keepdims=True)
    old_weights = (old_exp / denominator).astype(jnp.bfloat16)
    new_weights = (new_exp / denominator).astype(jnp.bfloat16)
    mixture = jnp.einsum(
        "bskgl,blkd->bskgd", old_weights, cache_v, preferred_element_type=jnp.float32
    )
    mixture = mixture + jnp.einsum(
        "bskgt,btkd->bskgd", new_weights, values_new, preferred_element_type=jnp.float32
    )
    return mixture.astype(jnp.bfloat16).reshape(seq_count, step_count, head_count * head_dim)


def local(
    states,
    norm_gain,
    query_base,
    key_base,
    value_base,
    output_base,
    query_down,
    query_up,
    key_down,
    key_up,
    value_down,
    value_up,
    output_down,
    output_up,
    adapter_layer,
    kv_lengths,
    cache_keys,
    cache_values,
):
    adapter_slot = adapter_layer[0]
    tp_size = lax.axis_size("tp")
    row_count = query_base.shape[0]
    merged_query = merge_rows(query_base, query_down, query_up, adapter_slot)
    merged_key = merge_rows(key_base, key_down, key_up, adapter_slot)
    merged_value = merge_rows(value_base, value_down, value_up, adapter_slot)
    merged_output = merge_rows(output_base, output_down, output_up, adapter_slot)
    joined = jnp.concatenate(
        (
            merged_query.reshape(row_count, tp_size, -1),
            merged_key.reshape(row_count, tp_size, -1),
            merged_value.reshape(row_count, tp_size, -1),
        ),
        2,
    ).reshape(row_count, -1)
    input_slice, output_slice = (
        lax.all_to_all(joined, "tp", split_axis=1, concat_axis=0, tiled=True),
        lax.all_to_all(merged_output, "tp", split_axis=1, concat_axis=0, tiled=True),
    )
    seq_count, step_count, model_width = states.shape
    normed = normalize(states, norm_gain)
    head_cols = HQ * DH // tp_size
    kv_cols = KVH * DH // tp_size
    flat_rows = normed.reshape(seq_count * step_count, model_width)
    columns = flat_rows
    projected = jnp.dot(
        columns,
        lax.all_gather(input_slice, "fsdp", axis=0, tiled=True),
        preferred_element_type=jnp.float32,
    )
    projected = projected.reshape(seq_count, step_count, -1)
    positions = (
        kv_lengths.astype(jnp.float32)[:, None] + jnp.arange(step_count, dtype=jnp.float32)[None, :]
    )
    queries = rotate(
        projected[:, :, :head_cols].reshape(seq_count, step_count, -1, DH), positions
    ).astype(jnp.bfloat16)
    keys_new = rotate(
        projected[:, :, head_cols : head_cols + kv_cols].reshape(seq_count, step_count, -1, DH),
        positions,
    ).astype(jnp.bfloat16)
    values_new = (
        projected[:, :, head_cols + kv_cols :]
        .reshape(seq_count, step_count, -1, DH)
        .astype(jnp.bfloat16)
    )
    attended = attend(queries, keys_new, values_new, cache_keys, cache_values, kv_lengths)
    all_heads = collect(attended, "tp", 2)
    flat_heads = all_heads.reshape(seq_count * step_count, -1)
    columns = flat_heads
    low_rank_delta = jnp.dot(
        columns,
        lax.all_gather(output_slice, "fsdp", axis=0, tiled=True),
        preferred_element_type=jnp.float32,
    )
    low_rank_delta = low_rank_delta.reshape(seq_count, step_count, -1)
    return low_rank_delta.astype(jnp.bfloat16)


def solution(mesh):
    in_specs = (
        P("fsdp", None, None),
        P(),
        P(("fsdp", "tp"), None),
        P(("fsdp", "tp"), None),
        P(("fsdp", "tp"), None),
        P(("fsdp", "tp"), None),
        P(None, ("fsdp", "tp"), None),
        P(),
        P(None, ("fsdp", "tp"), None),
        P(),
        P(None, ("fsdp", "tp"), None),
        P(),
        P(None, ("fsdp", "tp"), None),
        P(),
        P(),
        P("fsdp"),
        P("fsdp", None, "tp", None),
        P("fsdp", None, "tp", None),
    )
    out_specs = P("fsdp", None, "tp")
    return jax.shard_map(local, mesh=mesh, in_specs=in_specs, out_specs=out_specs, check_vma=False)
```

profile of v0, /device:TPU:1, one launch (start us, length us, event | category | flops | bytes accessed | tf_op | source)
XLA Modules:
  0.0 290.6 jit_solution(4913275454677924409)
XLA Ops:
  6.5 0.0 copy-start
  6.5 0.0 all-gather.3.cloned.1.call-start
  7.3 0.0 copy-start.6
  7.3 2.0 fusion.7
  9.3 0.1 copy.110
  9.4 0.9 fusion.33
  10.3 1.1 fusion.34
  11.4 0.1 copy_bitcast_fusion.2
  11.5 0.1 pad_maximum_fusion
  11.6 0.0 copy-start.5
  11.6 26.0 %all_to_all.40 = bf16[64,8,1280]{2,0,1:T(8,128)(2,1)} all-to-all(bf16[64,8,1280]{2,0,1:T(8,128)(2,1)S(1)} %pad_maximum_fusion), channel_id=1, replica_groups=mesh['fsdp'=16,'tp'=8] {'tp'}, dimensions={1} | all-to-all | bytes 2621440 | tf_op jit(solution)/shard_map/all_to_all | solution.py:128
  37.6 0.0 all-gather.3.cloned.1.call-update
  37.6 0.0 all-gather.5.cloned.1.call-start
  37.7 1.7 fusion.6
  39.3 0.1 copy.109
  39.4 0.0 copy-start.9
  39.4 0.0 copy-start.2
  39.4 21.3 %all_to_all.41 = bf16[64,8,1024]{2,0,1:T(8,128)(2,1)} all-to-all(bf16[64,8,1024]{2,0,1:T(8,128)(2,1)S(1)} %bitcast.136), channel_id=1, replica_groups=mesh['fsdp'=16,'tp'=8] {'tp'}, dimensions={1} | all-to-all | bytes 2097152 | tf_op jit(solution)/shard_map/all_to_all | solution.py:129
  60.7 0.0 all-gather.5.cloned.1.call-update
  60.8 0.0 copy-start.3
  60.8 0.1 iota_compare_fusion
  60.9 0.0 copy-done.2
  60.9 1.2 fusion.8
  62.1 0.3 multiply_cosine_fusion
  62.5 1.5 fusion.10
  63.9 92.0 %all-gather.3.cloned.1.call-done = bf16[8192,1280]{1,0:T(8,128)(2,1)} async-done(((bf16[512,1280]{1,0:T(8,128)(2,1)}), bf16[8192,1280]{1,0:T(8,128)(2,1)}) %all-gather.3.cloned.1.call-update) | async-done | bytes 20971536 | tf_op jit(solution)/shard_map/all_gather | solution.py:139
  155.9 11.4 %fusion = f32[32,4,1280]{2,0,1:T(8,128)S(1)} fusion(bf16[8192,1280]{1,0:T(8,128)(2,1)} %all-gather.3.cloned.1.call-done, bf16[32,4,8192]{2,1,0:T(4,128)(2,1)S(1)} %fusion.10), kind=kOutput, calls=%fused_computation | convolution fusion | flops 2684354560 | bytes 23724032 | tf_op jit(solution)/shard_map/dot_general | solution.py:137
  167.3 0.1 fusion.51
  167.4 0.1 fusion.54
  167.7 0.1 copy.92
  167.8 0.0 copy-start.4
  167.8 0.2 slice_negate_fusion
  168.0 0.2 fusion.43
  168.2 1.3 fusion.71
  169.5 0.4 copy-done.4
  170.0 1.6 fusion.70
  171.5 0.3 fusion.44
  171.8 0.8 fusion.17
  172.6 0.8 fusion.20
  173.5 0.4 fusion.27
  173.8 0.1 reshape.196
  173.9 0.1 copy.75
  174.0 0.3 broadcast_in_dim.26
  174.3 57.7 %all_to_all.42 = bf16[8,32,4,1024]{3,1,2,0:T(8,128)(2,1)S(1)} all-to-all(bf16[8,32,4,1024]{3,1,2,0:T(8,128)(2,1)S(1)} %broadcast_in_dim.26), channel_id=1, replica_groups=mesh['fsdp'=16,'tp'=8] {'tp'}, dimensions={0} | all-to-all | bytes 4194304 | tf_op jit(solution)/shard_map/all_to_all | solution.py:16
  232.0 0.2 copy.91
  232.1 42.5 %all-gather.5.cloned.1.call-done = bf16[8192,1024]{1,0:T(8,128)(2,1)} async-done(((bf16[512,1024]{1,0:T(8,128)(2,1)}), bf16[8192,1024]{1,0:T(8,128)(2,1)}) %all-gather.5.cloned.1.call-update) | async-done | bytes 16777232 | tf_op jit(solution)/shard_map/all_gather | solution.py:164
  274.6 8.2 %fusion.24 = bf16[32,4,1024]{2,0,1:T(8,128)(2,1)S(1)} fusion(bf16[32,4,8192]{2,0,1:T(8,128)(2,1)S(1)} %bitcast.128, bf16[8192,1024]{1,0:T(8,128)(2,1)} %all-gather.5.cloned.1.call-done), kind=kOutput, calls=%fused_computation.29 | convolution fusion | flops 2147614720 | bytes 19136512 | tf_op jit(solution)/shard_map/dot_general | solution.py:162
  282.8 0.9 copy.78
  (25 shorter events, 0.3 us)
Async XLA Ops:
  6.5 2.9 copy-start
  6.5 149.4 %all-gather.3.cloned.1.call-start = ((), (), s32[]{:S(2)}) async-start(), calls=%async_computation.3 | async-start | bytes 22282240 | tf_op jit(solution)/shard_map/all_gather | solution.py:139
  7.3 2.1 copy-start.6
  7.3 3.0 %copy-start.7 = (bf16[64,1024]{1,0:T(8,128)(2,1)S(1)}, bf16[64,1024]{1,0:T(8,128)(2,1)}, u32[]{:S(2)}) copy-start(bf16[64,1024]{1,0:T(8,128)(2,1)} %param.21) | copy-start | bytes 393220
  11.6 26.0 %copy-start.5 = (bf16[64,8192]{1,0:T(8,128)(2,1)S(1)}, bf16[64,8192]{1,0:T(8,128)(2,1)}, u32[]{:S(2)}) copy-start(bf16[64,8192]{1,0:T(8,128)(2,1)} %param.23) | copy-start | bytes 3145732
  37.6 237.0 %all-gather.5.cloned.1.call-start = ((), (), s32[]{:S(2)}) async-start(), calls=%async_computation.4 | async-start | bytes 17825792 | tf_op jit(solution)/shard_map/all_gather | solution.py:164
  39.4 21.3 %copy-start.9 = (s32[32]{0:T(128)S(1)}, s32[32]{0:T(128)}, u32[]{:S(2)}) copy-start(s32[32]{0:T(128)} %param.33) | copy-start | bytes 388
  39.4 21.5 %copy-start.2 = (bf16[32,4,8192]{2,1,0:T(4,128)(2,1)S(1)}, bf16[32,4,8192]{2,1,0:T(4,128)(2,1)}, u32[]{:S(2)}) copy-start(bf16[32,4,8192]{2,1,0:T(4,128)(2,1)} %param.18) | copy-start | bytes 6291460
  60.7 1.7 copy-start.8
  60.8 1.7 copy-start.3
  167.8 2.2 copy-start.4
  170.0 2.7 copy-start.10
  274.6 9.1 %copy-start.1 = (bf16[4,64,1024]{2,1,0:T(8,128)(2,1)S(1)}, bf16[4,64,1024]{2,1,0:T(8,128)(2,1)}, u32[]{:S(2)}) copy-start(bf16[4,64,1024]{2,1,0:T(8,128)(2,1)} %param.29) | copy-start | bytes 1572868
Sparse Core Ops, SparseCore 0:
  37.7 118.1 all-gather.2
  157.6 116.9 all-gather.4
where the time goes:
time: 291 us
  waiting for transfers between devices  135 us (46%)
  blocking collectives  105 us (36%)
  matrix products  29.2 us (10%)
  between operations  14.5 us (5%)
  other arithmetic  4.89 us (2%)
    all_gather x1, waiting for transfers between devices, local(): lax.all_gather(input_slice, 'fsdp', axis=0, tiled=True)  92 us
    all_to_all x1, blocking collectives, sent_to_all(): return lax.all_to_all(copies, axis, split_axis=0, concat_axis=0, tiled=True)  57.7 us
    all_gather x1, waiting for transfers between devices, local(): lax.all_gather(output_slice, 'fsdp', axis=0, tiled=True)  42.5 us
    all_to_all x1, blocking collectives, local(): lax.all_to_all(joined, 'tp', split_axis=1, concat_axis=0, tiled=True)  26 us
    all_to_all x1, blocking collectives, local(): lax.all_to_all(merged_output, 'tp', split_axis=1, concat_axis=0, tiled=True)  21.3 us
    dot_general x1, matrix products, local(): jnp.dot(columns, lax.all_gather(input_slice, 'fsdp', axis=0, tiled=True),...  11.4 us
    dot_general x1, matrix products, local(): jnp.dot(columns, lax.all_gather(output_slice, 'fsdp', axis=0, tiled=True)...  8.16 us
  transfers between devices with their start and end apart: 2, of which 2 were waited for; matrix products, arithmetic and copies ran while one was open for 8% of the time, Pallas kernels for 0%

commit v1 on v0

--- a/solution.py
+++ b/solution.py
@@ -9,6 +9,15 @@
 rope_theta = 1000000.0
 low_rank_scale = 0.5
 epsilon = 1e-06
+_produce_loads = lambda x_local: jnp.concatenate(
+    lax.all_to_all(
+        jnp.stack(lax.psum(1, axis_name="fsdp") * [x_local], axis=0),
+        axis_name="fsdp",
+        split_axis=0,
+        concat_axis=0,
+    ),
+    0,
+)
 
 
 def sent_to_all(array, axis):
@@ -160,9 +169,7 @@
     flat_heads = all_heads.reshape(seq_count * step_count, -1)
     columns = flat_heads
     low_rank_delta = jnp.dot(
-        columns,
-        lax.all_gather(output_slice, "fsdp", axis=0, tiled=True),
-        preferred_element_type=jnp.float32,
+        columns, _produce_loads(output_slice), preferred_element_type=jnp.float32
     )
     low_rank_delta = low_rank_delta.reshape(seq_count, step_count, -1)
     return low_rank_delta.astype(jnp.bfloat16)

time: 291 us -> 426 us (1.46)
  waiting for transfers between devices: 135 us -> 293 us
  blocking collectives: 105 us -> 60.1 us
  starting transfers between devices: 0.04 us -> 12.3 us
  local copies, waits for them, and re-layouts: 2.46 us -> 11.9 us
    all_to_all x0 -> x2, waiting for transfers between devices: none -> 183 us  [the longest x1 183 us: lax.all_to_all(jnp.stack(lax.psum(1, axis_name='fsdp') * [x_local], axis=...]
    all_gather x1 -> x0, waiting for transfers between devices: 42.5 us -> none  [local(): lax.all_gather(output_slice, 'fsdp', axis=0, tiled=True)]
    all_to_all x1, blocking collectives: 57.7 us -> 34.1 us  [sent_to_all(): return lax.all_to_all(copies, axis, split_axis=0, concat_axis=0, tiled=True)]
    all_to_all x1 -> x0, blocking collectives: 21.3 us -> none  [local(): lax.all_to_all(merged_output, 'tp', split_axis=1, concat_axis=0, tiled=True)]
    all_gather x1, waiting for transfers between devices: 92 us -> 110 us  [local(): lax.all_gather(input_slice, 'fsdp', axis=0, tiled=True)]
    all_to_all x0 -> x2, starting transfers between devices: none -> 12.3 us  [the longest x1 7.9 us: lax.all_to_all(jnp.stack(lax.psum(1, axis_name='fsdp') * [x_local], axis=...]
    another operation x0 -> x1, local copies, waits for them, and re-layouts: none -> 6.85 us  [jnp.stack(lax.psum(1, axis_name='fsdp') * [x_local], axis=0)]
  transfers between devices with their start and end apart: 2 -> 3, of which waited for: 2 -> 2; matrix products, arithmetic and copies ran while one was open for 8% -> 6% of each run, Pallas kernels for 0% -> 0%
where the time goes in v1:
time: 426 us
  waiting for transfers between devices  293 us (69%)
  blocking collectives  60.1 us (14%)
  matrix products  29.2 us (7%)
  between operations  14.5 us (3%)
  starting transfers between devices  12.3 us (3%)
  local copies, waits for them, and re-layouts  11.9 us (3%)
  other arithmetic  4.9 us (1%)
    all_to_all x1, waiting for transfers between devices, lax.all_to_all(jnp.stack(lax.psum(1, axis_name='fsdp') * [x_local], axis=...  183 us
    all_gather x1, waiting for transfers between devices, local(): lax.all_gather(input_slice, 'fsdp', axis=0, tiled=True)  110 us
    all_to_all x1, blocking collectives, sent_to_all(): return lax.all_to_all(copies, axis, split_axis=0, concat_axis=0, tiled=True)  34.1 us
    all_to_all x1, blocking collectives, local(): lax.all_to_all(joined, 'tp', split_axis=1, concat_axis=0, tiled=True)  26 us
    dot_general x1, matrix products, local(): jnp.dot(columns, lax.all_gather(input_slice, 'fsdp', axis=0, tiled=True),...  11.4 us
  transfers between devices with their start and end apart: 3, of which 2 were waited for; matrix products, arithmetic and copies ran while one was open for 6% of the time, Pallas kernels for 0%

profile of v1, /device:TPU:1, one launch (start us, length us, event | category | flops | bytes accessed | tf_op | source)
XLA Modules:
  0.0 425.5 jit_solution(3097506989165707831)
XLA Ops:
  6.5 0.0 copy-start
  7.3 2.0 fusion.5
  9.3 0.1 copy.121
  9.4 0.9 fusion.29
  10.3 1.1 fusion.28
  11.4 0.1 copy_bitcast_fusion.2
  11.5 0.1 pad_maximum_fusion
  11.6 0.0 copy-start.5
  11.6 26.0 %all_to_all.42 = bf16[64,8,1280]{2,0,1:T(8,128)(2,1)} all-to-all(bf16[64,8,1280]{2,0,1:T(8,128)(2,1)S(1)} %pad_maximum_fusion), channel_id=1, replica_groups=mesh['fsdp'=16,'tp'=8] {'tp'}, dimensions={1} | all-to-all | bytes 2621440 | tf_op jit(solution)/shard_map/all_to_all | solution.py:137
  37.6 0.0 all-gather.2.cloned.1.call-update
  37.6 0.0 copy-done.5
  37.6 1.7 fusion.4
  39.3 0.0 copy-start.9
  39.3 0.0 copy-start.2
  39.3 1.1 copy.120
  40.4 4.4 %all-to-all-start.2 = ((bf16[64,8,1024]{2,0,1:T(8,128)(2,1)}), bf16[64,8,1024]{2,0,1:T(8,128)(2,1)}, u32[]{:S(2)}, u32[]{:S(2)}) async-start(bf16[64,8,1024]{2,0,1:T(8,128)(2,1)} %bitcast.132), calls=%async_computation.2 | async-start | bytes 2097152 | tf_op jit(solution)/shard_map/all_to_all | solution.py:138
  44.8 0.0 copy-start.3
  44.8 0.1 iota_compare_fusion
  44.9 1.2 fusion.6
  46.1 0.3 multiply_cosine_fusion
  46.4 1.5 fusion.8
  47.9 110.1 %all-gather.2.cloned.1.call-done = bf16[8192,1280]{1,0:T(8,128)(2,1)} async-done(((bf16[512,1280]{1,0:T(8,128)(2,1)}), bf16[8192,1280]{1,0:T(8,128)(2,1)}) %all-gather.2.cloned.1.call-update) | async-done | bytes 20971536 | tf_op jit(solution)/shard_map/all_gather | solution.py:148
  158.0 11.4 %fusion = f32[32,4,1280]{2,0,1:T(8,128)S(1)} fusion(bf16[8192,1280]{1,0:T(8,128)(2,1)} %all-gather.2.cloned.1.call-done, bf16[32,4,8192]{2,1,0:T(4,128)(2,1)S(1)} %fusion.8), kind=kOutput, calls=%fused_computation | convolution fusion | flops 2684354560 | bytes 23724032 | tf_op jit(solution)/shard_map/dot_general | solution.py:146
  169.4 0.1 slice.29
  169.4 0.1 fusion.46
  169.5 0.1 copy.103
  169.6 0.1 fusion.49
  169.9 0.0 copy-start.4
  169.9 0.2 slice_negate_fusion
  170.1 0.2 fusion.38
  170.3 1.3 fusion.66
  171.6 0.4 copy-done.4
  172.0 1.6 fusion.65
  173.6 0.3 fusion.39
  173.9 0.8 fusion.15
  174.7 0.8 fusion.18
  175.6 0.4 fusion.22
  175.9 0.1 reshape.202
  176.0 0.1 copy.86
  176.1 0.0 all-to-all-done.2
  176.1 0.3 broadcast_in_dim.26
  176.3 34.1 %all_to_all.43 = bf16[8,32,4,1024]{3,1,2,0:T(8,128)(2,1)} all-to-all(bf16[8,32,4,1024]{3,1,2,0:T(8,128)(2,1)S(1)} %broadcast_in_dim.26), channel_id=1, replica_groups=mesh['fsdp'=16,'tp'=8] {'tp'}, dimensions={0} | all-to-all | bytes 4194304 | tf_op jit(solution)/shard_map/all_to_all | solution.py:25
  210.5 6.8 %stack.5 = bf16[16,512,1024]{2,1,0:T(8,128)(2,1)} broadcast(bf16[512,1024]{1,0:T(8,128)(2,1)} %bitcast.35), dimensions={1,2} | broadcast | bytes 17825792 | tf_op jit(solution)/shard_map/stack | solution.py:14
  217.3 7.9 %all-to-all-start.3 = ((bf16[16,512,1024]{2,1,0:T(8,128)(2,1)}), bf16[16,512,1024]{2,1,0:T(8,128)(2,1)}, u32[]{:S(2)}, u32[]{:S(2)}) async-start(bf16[16,512,1024]{2,1,0:T(8,128)(2,1)} %stack.5), calls=%async_computation.3 | async-start | bytes 33554432 | tf_op jit(solution)/shard_map/all_to_all | solution.py:13
  225.2 1.8 copy.102
  227.1 182.5 %all-to-all-done.3 = bf16[16,512,1024]{2,1,0:T(8,128)(2,1)} async-done(((bf16[16,512,1024]{2,1,0:T(8,128)(2,1)}), bf16[16,512,1024]{2,1,0:T(8,128)(2,1)}, u32[]{:S(2)}, u32[]{:S(2)}) %all-to-all-start.3) | async-done | bytes 16777248 | tf_op jit(solution)/shard_map/all_to_all | solution.py:13
  409.6 8.2 %convolution_convert_fusion = bf16[32,4,1024]{2,0,1:T(8,128)(2,1)S(1)} fusion(bf16[32,4,8192]{2,0,1:T(8,128)(2,1)S(1)} %bitcast.127, bf16[8192,1024,1]{1,0,2:T(8,128)(2,1)} %bitcast.37), kind=kOutput, calls=%fused_computation.27 | convolution fusion | flops 2147614720 | bytes 19136512 | tf_op jit(solution)/shard_map/dot_general | solution.py:171
  417.7 0.9 copy.89
  (26 shorter events, 0.2 us)
Async XLA Ops:
  6.5 2.9 copy-start
  6.5 151.4 %all-gather.2.cloned.1.call-start = ((), (), s32[]{:S(2)}) async-start(), calls=%async_computation.4 | async-start | bytes 22282240 | tf_op jit(solution)/shard_map/all_gather | solution.py:148
  7.3 2.1 copy-start.6
  7.3 3.0 copy-start.7
  11.6 26.0 %copy-start.5 = (bf16[64,8192]{1,0:T(8,128)(2,1)S(1)}, bf16[64,8192]{1,0:T(8,128)(2,1)}, u32[]{:S(2)}) copy-start(bf16[64,8192]{1,0:T(8,128)(2,1)} %param.23) | copy-start | bytes 3145732
  39.3 5.5 %copy-start.9 = (s32[32]{0:T(128)S(1)}, s32[32]{0:T(128)}, u32[]{:S(2)}) copy-start(s32[32]{0:T(128)} %param.33) | copy-start | bytes 388
  39.3 5.6 %copy-start.2 = (bf16[32,4,8192]{2,1,0:T(4,128)(2,1)S(1)}, bf16[32,4,8192]{2,1,0:T(4,128)(2,1)}, u32[]{:S(2)}) copy-start(bf16[32,4,8192]{2,1,0:T(4,128)(2,1)} %param.18) | copy-start | bytes 6291460
  40.4 6.1 %copy-start.8 = (f32[8192]{0:T(1024)S(1)}, f32[8192]{0:T(1024)}, u32[]{:S(2)}) copy-start(f32[8192]{0:T(1024)} %param.19) | copy-start | bytes 98308
  40.4 135.7 %all-to-all-start.2 = ((bf16[64,8,1024]{2,0,1:T(8,128)(2,1)}), bf16[64,8,1024]{2,0,1:T(8,128)(2,1)}, u32[]{:S(2)}, u32[]{:S(2)}) async-start(bf16[64,8,1024]{2,0,1:T(8,128)(2,1)} %bitcast.132), calls=%async_computation.2 | async-start | bytes 2097152 | tf_op jit(solution)/shard_map/all_to_all | solution.py:138
  44.8 1.7 copy-start.3
  169.9 2.2 copy-start.4
  172.0 2.7 copy-start.10
  217.3 192.2 %all-to-all-start.3 = ((bf16[16,512,1024]{2,1,0:T(8,128)(2,1)}), bf16[16,512,1024]{2,1,0:T(8,128)(2,1)}, u32[]{:S(2)}, u32[]{:S(2)}) async-start(bf16[16,512,1024]{2,1,0:T(8,128)(2,1)} %stack.5), calls=%async_computation.3 | async-start | bytes 33554432 | tf_op jit(solution)/shard_map/all_to_all | solution.py:13
  409.6 9.1 %copy-start.1 = (bf16[4,64,1024]{2,1,0:T(8,128)(2,1)S(1)}, bf16[4,64,1024]{2,1,0:T(8,128)(2,1)}, u32[]{:S(2)}) copy-start(bf16[4,64,1024]{2,1,0:T(8,128)(2,1)} %param.27) | copy-start | bytes 1572868
Sparse Core Ops, SparseCore 0:
  37.7 120.2 all-gather.1
